TPU v7x, 256 devices: a whole 4x4x8 slice. The times are simulated.
256 devices in a mesh: dp: 8 (over z), tensor: 32 (over y, x, core).
Axes of the slice: x: 4, y: 4, z: 8, core: 2. Of those that a mesh axis runs over, the one named last changes fastest.
Arguments:
- hidden: bfloat16 [16384, 1536], P(('dp', 'tensor')), parts along dimension 0, may hold values from -6 to 6
- segment_ids: int32 [16384], P('dp'), parts along dimension 0, may hold values from 0 to 5, never falling along the last dimension, each value on 1 to 1024 neighbouring positions
- routes: int32 [16384, 8], P(('dp', 'tensor')), parts along dimension 0, may hold values from 0 to 39, all different within a row; in each aligned block of 512 rows (0 to 511, 512 to 1023, ...) at most 204 rows name the same one
- route_weights: bfloat16 [16384, 8], P(('dp', 'tensor')), parts along dimension 0, may hold values from 0.099609375 to 1
- attn_gain: float32 [1536], replicated, may hold values from 0.1 to 1.9
- w_qkv: bfloat16 [1536, 2560], P(None, 'tensor')
- w_out: bfloat16 [1536, 1536], P(None, 'tensor'), may hold values from -0.15625 to 0.15625
- ffn_gain: float32 [1536], replicated, may hold values from 0.1 to 1.9
- w_gate_up: bfloat16 [160, 1536, 256], P('tensor'), may hold values from -0.15625 to 0.15625
- w_down: bfloat16 [160, 128, 1536], P('tensor'), may hold values from -0.25 to 0.25
Outputs:
- after_attention: bfloat16 [16384, 1536], P(('dp', 'tensor')), parts along dimension 0
- hidden_out: bfloat16 [16384, 1536], P(('dp', 'tensor')), parts along dimension 0
- kv_cache: bfloat16 [32, 4096, 128], P('tensor', 'dp'), parts along dimension 1
There are 8 independent parts, one for each index of `dp`. A program takes and returns all parts, laid end to end along the dimension named above; an argument that names none is the same for every part. Nothing has to cross between parts.
Inputs may be any that keep to these rules, and one draw needn't show every extreme that they name: `segment_ids`: prompt numbers never fall along the sequence; each prompt has 1 to 1024 tokens, one exactly 1024. `routes`: each token names 8 different experts. In each aligned block of 512 tokens no expert is named by more than 204 tokens, a bound that some block reaches.
All inputs are finite; a program needn't handle non-finite values.
Results may differ from a plain program's by a relative error of at most 0.0075.
Values may be sent and summed in bfloat16 or wider, within the bound.
A program may use at most 128 MiB of HBM per device.

v0:
```python
import math
import jax
import jax.numpy as jnp
from jax import lax
from jax.sharding import PartitionSpec as P

KVH = 8
HD = 64
GQ = 3
attn_scale = 0.015625
residual_scale = 0.22
rope_base = 10000.0
norm_eps = 1e-06
masked_floor = -1e30


def partner(value, axis, apart):
    mask = 2**apart
    pairs = [(source, source ^ mask) for source in range(lax.axis_size(axis))]
    return lax.ppermute(value, axis, pairs)


def rms_norm(row_block, gain_row):
    widened = row_block.astype(jnp.float32)
    mean_square = jnp.mean(widened * widened, axis=-1, keepdims=True)
    return (widened * lax.rsqrt(mean_square + norm_eps) * gain_row).astype(jnp.bfloat16)


def segment_starts(segment_ids):
    places = jnp.arange(segment_ids.shape[0], dtype=jnp.int32)
    earlier = jnp.concatenate([segment_ids[:1] - 1, segment_ids[:-1]])
    boundary = jnp.where(segment_ids != earlier, places, jnp.zeros_like(places))
    return lax.cummax(boundary, axis=0)


def rotate(vectors, positions):
    half_width = vectors.shape[-1] // 2
    freq_steps = jnp.arange(half_width, dtype=jnp.float32)
    frequency = jnp.exp(freq_steps * (-2.0 * math.log(rope_base) / vectors.shape[-1]))
    angles = positions.astype(jnp.float32)[:, None] * frequency[None, :]
    cosine = jnp.cos(angles)[:, None, :]
    sine_part = jnp.sin(angles)[:, None, :]
    first_half = vectors[..., :half_width]
    second_half = vectors[..., half_width:]
    return jnp.concatenate(
        [
            first_half * cosine - second_half * sine_part,
            second_half * cosine + first_half * sine_part,
        ],
        axis=-1,
    )


def gather_levels(parts, level_bits, join_axes, sender):
    index_now = lax.axis_index("tensor")
    for level_bit in level_bits:
        arrived = sender(parts, level_bit)
        is_upper = index_now >> level_bit & 1 == 1
        joined_parts = []
        for own_part, peer_part, join_axis in zip(parts, arrived, join_axes):
            lower_first = jnp.concatenate([own_part, peer_part], join_axis)
            upper_first = jnp.concatenate([peer_part, own_part], join_axis)
            joined_parts.append(jnp.where(is_upper, upper_first, lower_first))
        parts = tuple(joined_parts)
    return parts


def fold_levels(partial_sum, level_bits, sender):
    index_now = lax.axis_index("tensor")
    for level_bit in reversed(level_bits):
        half_rows = partial_sum.shape[0] // 2
        lower_rows = partial_sum[:half_rows]
        upper_rows = partial_sum[half_rows:]
        is_upper = index_now >> level_bit & 1 == 1
        kept_rows = jnp.where(is_upper, upper_rows, lower_rows)
        sent_rows = jnp.where(is_upper, lower_rows, upper_rows)
        partial_sum = kept_rows + sender(sent_rows, level_bit)
    return partial_sum


def project_pairs(row_block, w_pairs, positions):
    head_size = w_pairs.shape[1] // 2
    paired = jnp.dot(row_block, w_pairs, preferred_element_type=jnp.float32)
    rotated = rotate(paired[:, None, :head_size], positions)[:, 0]
    return jnp.concatenate([rotated, paired[:, head_size:]], axis=1).astype(jnp.bfloat16)


def expert_term(inputs, routes, route_weights, gate_up, down_proj, first_expert, capacity):
    row_count = inputs.shape[0]
    model_width = inputs.shape[1]
    expert_count = gate_up.shape[0]
    inner_width = down_proj.shape[1]
    expert_ids = first_expert + jnp.arange(expert_count, dtype=jnp.int32)
    matches = routes[:, None, :] == expert_ids[None, :, None]
    chosen = jnp.any(matches, axis=2)
    shares = jnp.sum(jnp.where(matches, route_weights.astype(jnp.float32)[:, None, :], 0.0), axis=2)
    ranks = jnp.cumsum(chosen.astype(jnp.int32), axis=0) - 1
    targets = jnp.where(chosen, ranks, capacity)
    row_ids = jnp.broadcast_to(
        jnp.arange(row_count, dtype=jnp.int32)[:, None], (row_count, expert_count)
    )
    column_ids = jnp.broadcast_to(
        jnp.arange(expert_count, dtype=jnp.int32)[None, :], (row_count, expert_count)
    )
    slot_table = (
        jnp.full((expert_count, capacity + 1), row_count, jnp.int32)
        .at[column_ids, targets]
        .set(row_ids)[:, :capacity]
    )
    padded_in = jnp.concatenate([inputs, jnp.zeros((1, model_width), inputs.dtype)], axis=0)
    padded_share = jnp.concatenate([shares, jnp.zeros((1, expert_count), jnp.float32)], axis=0)
    picked = padded_in[slot_table]
    slot_share = jnp.take_along_axis(padded_share.T, slot_table, axis=1)
    gate_up_out = jnp.einsum("ecd,edf->ecf", picked, gate_up, preferred_element_type=jnp.float32)
    inner_act = (
        jax.nn.silu(gate_up_out[..., :inner_width]) * gate_up_out[..., inner_width:]
    ).astype(jnp.bfloat16)
    produced = (
        jnp.einsum("ecf,efd->ecd", inner_act, down_proj, preferred_element_type=jnp.float32)
        * slot_share[..., None]
    )
    summed = (
        jnp.zeros((row_count + 1, model_width), jnp.float32)
        .at[slot_table.reshape(-1)]
        .add(produced.reshape(-1, model_width))
    )
    return summed[:row_count]


def on_device(
    hidden, segment_ids, routes, route_weights, attn_gain, w_qkv, w_out, ffn_gain, w_gate_up, w_down
):
    device_count = lax.axis_size("tensor")
    quarters = device_count // KVH
    index_now = lax.axis_index("tensor")
    quarter_index = index_now // KVH
    group_index = index_now % KVH
    group_bits = list(range(KVH.bit_length() - 1))
    quarter_bits = list(range(len(group_bits), device_count.bit_length() - 1))
    seq_len = segment_ids.shape[0]
    rows_quarter = seq_len // quarters
    model_width = hidden.shape[1]
    starts = segment_starts(segment_ids)
    positions = jnp.arange(seq_len, dtype=jnp.int32) - starts
    own_positions = lax.dynamic_slice_in_dim(
        positions, quarter_index * rows_quarter, rows_quarter, 0
    )
    normed = rms_norm(hidden, attn_gain)
    qkv_width = w_qkv.shape[1]
    joined = jnp.concatenate([w_qkv, w_out], axis=1)
    (gathered_cols,) = gather_levels(
        (joined,),
        quarter_bits,
        (1,),
        lambda payload, level_bit: (partner(payload[0], "tensor", level_bit),),
    )
    by_quarter = gathered_cols.reshape(model_width, quarters, joined.shape[1])
    w_group = by_quarter[:, :, :qkv_width].reshape(model_width, quarters * qkv_width)
    w_attn_out = by_quarter[:, :, qkv_width:].reshape(model_width, GQ * HD)
    w_query = w_group[:, : GQ * HD]
    w_pairs = w_group[:, GQ * HD :]
    all_rows = lax.all_gather(normed, "tensor", axis=0, tiled=True)
    own_rows = lax.dynamic_slice_in_dim(all_rows, quarter_index * rows_quarter, rows_quarter, 0)
    key_values = project_pairs(all_rows, w_pairs, positions)
    kv_block = lax.dynamic_slice_in_dim(key_values, quarter_index * rows_quarter, rows_quarter, 0)
    query_proj = jnp.dot(own_rows, w_query, preferred_element_type=jnp.float32).reshape(
        rows_quarter, GQ, HD
    )
    queries_heads = rotate(query_proj, own_positions).astype(jnp.bfloat16).transpose(1, 0, 2)
    block_rows = min(256, rows_quarter)
    key_block = min(512, seq_len)

    def attend(block_number):
        first_row = block_number * block_rows
        block_queries = lax.dynamic_slice_in_dim(queries_heads, first_row, block_rows, 1).reshape(
            GQ * block_rows, HD
        )
        first_place = quarter_index * rows_quarter + first_row
        query_places = first_place + jnp.arange(block_rows, dtype=jnp.int32)
        query_starts = lax.dynamic_slice_in_dim(starts, first_place, block_rows, 0)
        lowest = query_starts[0] // key_block
        highest = (first_place + block_rows - 1) // key_block + 1

        def step_keys(key_number, loop_state):
            row_peak, totals, accumulated = loop_state
            key_offset = key_number * key_block
            block_pairs = lax.dynamic_slice_in_dim(key_values, key_offset, key_block, 0)
            key_places = key_offset + jnp.arange(key_block, dtype=jnp.int32)
            allowed = (key_places[None, :] <= query_places[:, None]) & (
                key_places[None, :] >= query_starts[:, None]
            )
            scores = (
                lax.dot_general(
                    block_queries,
                    block_pairs[:, :HD],
                    (((1,), (1,)), ((), ())),
                    preferred_element_type=jnp.float32,
                )
                * attn_scale
            )
            scores = jnp.where(jnp.tile(allowed, (GQ, 1)), scores, -jnp.inf)
            new_peak = jnp.maximum(row_peak, jnp.max(scores, axis=1))
            weights = jnp.exp(scores - new_peak[:, None])
            factor = jnp.exp(row_peak - new_peak)
            totals = totals * factor + jnp.sum(weights, axis=1)
            accumulated = accumulated * factor[:, None] + jnp.dot(
                weights.astype(jnp.bfloat16),
                block_pairs[:, HD:],
                preferred_element_type=jnp.float32,
            )
            return (new_peak, totals, accumulated)

        start_state = (
            jnp.full((GQ * block_rows,), masked_floor, jnp.float32),
            jnp.zeros((GQ * block_rows,), jnp.float32),
            jnp.zeros((GQ * block_rows, HD), jnp.float32),
        )
        row_peak, totals, accumulated = lax.fori_loop(lowest, highest, step_keys, start_state)
        mixed = (accumulated / totals[:, None]).astype(jnp.bfloat16).reshape(GQ, block_rows, HD)
        return mixed.transpose(1, 0, 2).reshape(block_rows, GQ * HD)

    attended = lax.map(attend, jnp.arange(rows_quarter // block_rows, dtype=jnp.int32)).reshape(
        rows_quarter, GQ * HD
    )
    partial_proj = lax.dot_general(
        attended, w_attn_out, (((1,), (1,)), ((), ())), preferred_element_type=jnp.float32
    )
    projection = fold_levels(
        partial_proj,
        group_bits,
        lambda sent_rows, level_bit: partner(
            sent_rows.astype(jnp.bfloat16), "tensor", level_bit
        ).astype(sent_rows.dtype),
    )
    after_attention = (hidden.astype(jnp.float32) + residual_scale * projection).astype(
        jnp.bfloat16
    )
    expert_in = rms_norm(after_attention, ffn_gain)
    local_experts = w_gate_up.shape[0]
    capacity = 2 * rows_quarter // 5
    rows_all, routes_all, shares_all = (
        lax.all_gather(expert_in, "tensor", axis=0, tiled=True),
        lax.all_gather(routes, "tensor", axis=0, tiled=True),
        lax.all_gather(route_weights, "tensor", axis=0, tiled=True),
    )
    expert_part = expert_term(
        rows_all,
        routes_all,
        shares_all,
        w_gate_up,
        w_down,
        group_index * local_experts,
        quarters * capacity,
    )
    expert_sum = lax.psum_scatter(
        expert_part.astype(jnp.bfloat16), "tensor", scatter_dimension=0, tiled=True
    ).astype(jnp.float32)
    hidden_out = (after_attention.astype(jnp.float32) + residual_scale * expert_sum).astype(
        jnp.bfloat16
    )
    return (after_attention, hidden_out, kv_block[None])


def solution(mesh):
    placed = (
        P(("dp", "tensor"), None),
        P("dp"),
        P(("dp", "tensor"), None),
        P(("dp", "tensor"), None),
        P(),
        P(None, "tensor"),
        P(None, "tensor"),
        P(),
        P("tensor", None, None),
        P("tensor", None, None),
    )
    return jax.shard_map(
        on_device,
        mesh=mesh,
        in_specs=placed,
        out_specs=(P(("dp", "tensor"), None), P(("dp", "tensor"), None), P("tensor", "dp", None)),
        check_vma=False,
    )
```

profile of v0, /device:TPU:2, one launch (start us, length us, event | category | flops | bytes accessed | tf_op | source)
XLA Modules:
  0.0 499.2 jit_solution(2245536383037473471)
XLA Ops:
  8.4 1.7 fusion.19
  11.3 1.7 collective-permute-start
  16.1 6.1 %collective-permute-done = bf16[1536,128]{0,1:T(8,128)(2,1)S(1)} collective-permute-done((bf16[1536,128]{0,1:T(8,128)(2,1)S(1)}, bf16[1536,128]{0,1:T(8,128)(2,1)S(1)}, u32[]{:S(2)}, u32[]{:S(2)}) %collective-permute-start) | collective-permute-done | bytes 393248 | tf_op jit(solution)/shard_map/ppermute | solution.py:20
  23.6 3.3 collective-permute-start.1
  27.1 1.7 multiply_cosine_fusion.1
  28.8 18.0 %collective-permute-done.1 = bf16[1536,256]{0,1:T(8,128)(2,1)S(1)} collective-permute-done((bf16[1536,256]{0,1:T(8,128)(2,1)S(1)}, bf16[1536,256]{0,1:T(8,128)(2,1)S(1)}, u32[]{:S(2)}, u32[]{:S(2)}) %collective-permute-start.1) | collective-permute-done | bytes 786464 | tf_op jit(solution)/shard_map/ppermute | solution.py:20
  48.0 30.3 %all-gather.5.cloned.1.call-done = bf16[2048,1536]{1,0:T(8,128)(2,1)} async-done(((bf16[64,1536]{1,0:T(8,128)(2,1)}), bf16[2048,1536]{1,0:T(8,128)(2,1)}) %all-gather.5.cloned.1.call-update) | async-done | bytes 6291472 | tf_op jit(solution)/shard_map/all_gather | solution.py:162
  78.3 4.9 fusion.25
  83.3 2.1 fusion.12
  89.6 2.1 copy.61
  93.3 14.6 %while.59 = (s32[]{:T(128)}, bf16[2,256,192]{1,2,0:T(8,128)(2,1)}, s32[2]{0:T(128)S(1)}, s32[]{:T(128)}, s32[2048]{0:T(1024)S(1)}, /*index=5*/bf16[3,512,64]{2,1...) while((s32[]{:T(128)}, bf16[2,256,192]{1,2,0:T(8,128)(2,1)}, ...), condition=%wide.region_8.9_spmd, body=%wide.region_3.8_spmd.sunk | while | flops 104007976 | bytes 10327068 | solution.py:222
  97.8 2.0 while.60
  105.0 2.0 while.60
  108.8 1.7 fusion.47
  110.5 1.7 copy-done.1
  112.3 2.1 collective-permute-start.2
  114.4 19.2 %collective-permute-done.2 = bf16[256,1536]{1,0:T(8,128)(2,1)} collective-permute-done((bf16[256,1536]{1,0:T(8,128)(2,1)S(1)}, bf16[256,1536]{1,0:T(8,128)(2,1)}, u32[]{:S(2)}, u32[]{:S(2)}) %collective-permute-start.2) | collective-permute-done | bytes 786464 | tf_op jit(solution)/shard_map/ppermute | solution.py:20
  133.7 2.5 convert_add_fusion
  137.0 1.5 collective-permute-start.3
  138.5 9.2 %collective-permute-done.3 = bf16[128,1536]{1,0:T(8,128)(2,1)} collective-permute-done((bf16[128,1536]{1,0:T(8,128)(2,1)}, bf16[128,1536]{1,0:T(8,128)(2,1)}, u32[]{:S(2)}, u32[]{:S(2)}) %collective-permute-start.3) | collective-permute-done | bytes 393248 | tf_op jit(solution)/shard_map/ppermute | solution.py:20
  151.5 30.1 %all-gather.1 = bf16[32,64,8]{1,2,0:T(8,128)(2,1)S(1)} all-gather(bf16[1,64,8]{1,2,0:T(8,128)(2,1)S(1)} %bitcast.110), channel_id=1, replica_groups=mesh['dp'=8,'tensor'=32] {'tensor'}, dimensions={0}, use_global_device_ids=true | all-gather | bytes 33792 | tf_op jit(solution)/shard_map/all_gather | solution.py:244
  181.7 23.6 %all-gather = s32[32,64,8]{1,2,0:T(8,128)S(1)} all-gather(s32[1,64,8]{1,2,0:T(8,128)S(1)} %bitcast.109), channel_id=1, replica_groups=mesh['dp'=8,'tensor'=32] {'tensor'}, dimensions={0}, use_global_device_ids=true | all-gather | bytes 67584 | tf_op jit(solution)/shard_map/all_gather | solution.py:243
  211.2 37.9 %scatter_custom_fusion.1 = s32[4085]{0:T(1024)S(1)} fusion(s32[10240]{0:T(1024)S(1)} %reshape.400, s32[10240]{0:T(1024)S(1)} %reshape.402, s32[]{:T(128)} %constant.223.clone.1), kind=kCustom, calls=%fused_computation.101 | custom fusion | bytes 16344
  250.6 40.4 %gather_fusion.1 = f32[4080]{0:T(1024)S(1)} fusion(f32[5,2049]{0,1:T(8,128)S(1)} %pad_bitcast_fusion, s32[4080]{0:T(1024)S(1)} %reshape.386), kind=kCustom, calls=%fused_computation.1 | custom fusion | bytes 65280 | tf_op jit(solution)/shard_map/jit(take_along_axis)/gather | solution.py:113
  291.4 5.8 %concatenate.56 = bf16[2049,1536]{1,0:T(8,128)(2,1)} pad(bf16[2048,1536]{1,0:T(8,128)(2,1)} %all-gather.7.cloned.1.call-done, bf16[]{:T(256)} %constant.215.clone.1), padding=0_1x0_0 | pad | bytes 12585986 | tf_op jit(solution)/shard_map/concatenate | solution.py:110
  297.2 28.9 %gather_fusion = bf16[4080,1536]{1,0:T(8,128)(2,1)} fusion(bf16[2049,1536]{1,0:T(8,128)(2,1)} %concatenate.56, s32[4096]{0:T(1024)S(1)} %pad_clamp_fusion), kind=kCustom, calls=%fused_computation | custom fusion | bytes 25083840 | tf_op jit(solution)/shard_map/gather | solution.py:112
  326.2 7.6 %fusion.48 = f32[5,816,256]{2,1,0:T(8,128)S(1)} fusion(bf16[5,816,1536]{2,1,0:T(8,128)(2,1)} %bitcast.94, bf16[5,1536,256]{2,1,0:T(8,128)(2,1)} %param.22), kind=kOutput, calls=%fused_computation.117 | convolution fusion | flops 3208642560 | bytes 20643840 | tf_op jit(solution)/shard_map/ecd,edf->ecf/dot_general | solution.py:114
  333.8 10.1 %convolution_multiply_fusion = f32[5,816,1536]{2,1,0:T(8,128)} fusion(bf16[5,128,1536]{2,1,0:T(8,128)(2,1)S(1)} %copy-done, f32[5,816]{1,0:T(8,128)S(1)} %and_select_fusion, f32[5,816,256]{2,1,0:T(8,128)S(1)} %fusion.48), kind=kOutput, calls=%fused_computation.22 | convolution fusion | flops 1613721600 | bytes 31227840 | tf_op jit(solution)/shard_map/ecf,efd->ecd/dot_general | solution.py:119
  343.9 46.6 %scatter_custom_fusion = f32[2049,1536]{1,0:T(8,128)} fusion(s32[4080]{0:T(1024)S(1)} %bitcast.107, f32[4080,1536]{1,0:T(8,128)} %bitcast.92, f32[]{:T(128)} %constant.216.clone.1), kind=kCustom, calls=%fused_computation.24 | custom fusion | flops 6266880 | bytes 12589568 | tf_op jit(solution)/shard_map/scatter-add | solution.py:125
  390.5 8.0 %slice.188 = bf16[2048,1536]{1,0:T(8,128)(2,1)} slice(f32[2049,1536]{1,0:T(8,128)} %scatter_custom_fusion), slice={[0:2048], [0:1536]} | slice | bytes 12582912 | tf_op jit(solution)/shard_map/slice | solution.py:127
  400.3 90.7 %reduce-scatter.2.cloned.1.call-done = bf16[64,1536]{1,0:T(8,128)(2,1)} async-done(((bf16[2048,1536]{1,0:T(8,128)(2,1)}), bf16[64,1536]{1,0:T(8,128)(2,1)}) %reduce-scatter.2.cloned.1.call-update) | async-done | bytes 196624 | tf_op jit(solution)/shard_map/reduce_scatter | solution.py:255
  491.0 1.7 fusion.24
  (159 shorter events, 36.5 us)
Async XLA Ops:
  7.2 326.6 %copy-start = (bf16[5,128,1536]{2,1,0:T(8,128)(2,1)S(1)}, bf16[5,128,1536]{2,1,0:T(8,128)(2,1)}, u32[]{:S(2)}) copy-start(bf16[5,128,1536]{2,1,0:T(8,128)(2,1)} %param.23) | copy-start | bytes 5898244
  7.2 71.1 %all-gather.5.cloned.1.call-start = ((), (), s32[]{:S(2)}) async-start(), calls=%async_computation.1 | async-start | bytes 6488064 | tf_op jit(solution)/shard_map/all_gather | solution.py:162
  10.2 281.2 %all-gather.7.cloned.1.call-start = ((), (), s32[]{:S(2)}) async-start(), calls=%async_computation.2 | async-start | bytes 6488064 | tf_op jit(solution)/shard_map/all_gather | solution.py:242
  11.3 10.9 %collective-permute-start = (bf16[1536,128]{0,1:T(8,128)(2,1)S(1)}, bf16[1536,128]{0,1:T(8,128)(2,1)S(1)}, u32[]{:S(2)}, u32[]{:S(2)}) collective-permute-start(bf16[1536,128]{0,1:T(8,128)(2,1)S(1)} %pad_maximum_fusion.1), channel_id=1, source_target_pairs={{0,8},{1,9},{2,10},{3,11},{4,12},{5,13},{6,14},{7,15},{8,0},{9,1},... | collective-permute-start | bytes 1179656 | tf_op jit(solution)/shard_map/ppermute | solution.py:20
  23.6 23.2 %collective-permute-start.1 = (bf16[1536,256]{0,1:T(8,128)(2,1)S(1)}, bf16[1536,256]{0,1:T(8,128)(2,1)S(1)}, u32[]{:S(2)}, u32[]{:S(2)}) collective-permute-start(bf16[1536,256]{0,1:T(8,128)(2,1)S(1)} %maximum_select_fusion.1), channel_id=1, source_target_pairs={{0,16},{1,17},{2,18},{3,19},{4,20},{5,21},{6,22},{7,23},{8,24},{9,... | collective-permute-start | bytes 2359304 | tf_op jit(solution)/shard_map/ppermute | solution.py:20
  83.2 4.1 copy-start.2
  87.3 0.7 copy-start.4
  97.7 2.1 copy-start.8
  99.9 0.7 copy-start.9
  105.0 2.1 copy-start.8
  107.2 0.7 copy-start.9
  110.5 1.7 copy-start.1
  112.3 21.4 %collective-permute-start.2 = (bf16[256,1536]{1,0:T(8,128)(2,1)S(1)}, bf16[256,1536]{1,0:T(8,128)(2,1)}, u32[]{:S(2)}, u32[]{:S(2)}) collective-permute-start(bf16[256,1536]{1,0:T(8,128)(2,1)S(1)} %select_convert_fusion), channel_id=1, source_target_pairs={{0,4},{1,5},{2,6},{3,7},{4,0},{5,1},{6,2},{7,3},{8,12},{9,13},{10,... | collective-permute-start | bytes 2359304 | tf_op jit(solution)/shard_map/ppermute | solution.py:20
  137.0 10.7 %collective-permute-start.3 = (bf16[128,1536]{1,0:T(8,128)(2,1)}, bf16[128,1536]{1,0:T(8,128)(2,1)}, u32[]{:S(2)}, u32[]{:S(2)}) collective-permute-start(bf16[128,1536]{1,0:T(8,128)(2,1)} %select_convert_fusion.1), channel_id=1, source_target_pairs={{0,2},{1,3},{2,0},{3,1},{4,6},{5,7},{6,4},{7,5},{8,10},{9,11},{10,... | collective-permute-start | bytes 1179656 | tf_op jit(solution)/shard_map/ppermute | solution.py:20
  138.5 11.9 %copy-start.6 = (bf16[64,1536]{1,0:T(8,128)(2,1)S(1)}, bf16[64,1536]{1,0:T(8,128)(2,1)}, u32[]{:S(2)}) copy-start(bf16[64,1536]{1,0:T(8,128)(2,1)} %param.14) | copy-start | bytes 589828
  138.5 12.1 %copy-start.10 = (f32[1536]{0:T(1024)S(1)}, f32[1536]{0:T(1024)}, u32[]{:S(2)}) copy-start(f32[1536]{0:T(1024)} %param.21) | copy-start | bytes 18436
  138.5 13.0 %copy-start.12 = (bf16[64,8]{0,1:T(8,128)(2,1)S(1)}, bf16[64,8]{0,1:T(8,128)(2,1)}, u32[]{:S(2)}) copy-start(bf16[64,8]{0,1:T(8,128)(2,1)} %param.17) | copy-start | bytes 3076
  148.8 32.9 %copy-start.11 = (s32[64,8]{0,1:T(8,128)S(1)}, s32[64,8]{0,1:T(8,128)}, u32[]{:S(2)}) copy-start(s32[64,8]{0,1:T(8,128)} %param.16) | copy-start | bytes 6148
  148.8 58.8 %copy-start.14 = (s32[2]{0:T(128)S(1)}, s32[2]{0:T(128)}, u32[]{:S(2)}) copy-start(s32[2]{0:T(128)} %constant.248) | copy-start | bytes 28
  148.9 58.9 %copy-start.13 = (s32[2]{0:T(128)S(1)}, s32[2]{0:T(128)}, u32[]{:S(2)}) copy-start(s32[2]{0:T(128)} %constant.251) | copy-start | bytes 28
  148.9 1.5 collective-permute-start.4
  150.6 340.4 %copy-start.7 = (bf16[64,1536]{1,0:T(8,128)(2,1)}, bf16[64,1536]{1,0:T(8,128)(2,1)S(1)}, u32[]{:S(2)}) copy-start(bf16[64,1536]{1,0:T(8,128)(2,1)S(1)} %get-tuple-element.314) | copy-start | bytes 589828
  151.5 339.5 %reduce-scatter.2.cloned.1.call-start = ((), (), s32[]{:S(2)}) async-start(), calls=%async_computation.3 | async-start | bytes 6488064 | tf_op jit(solution)/shard_map/reduce_scatter | solution.py:255
  398.5 0.9 copy-start.3
  398.5 1.0 copy-start.5
Sparse Core Ops, SparseCore 0:
  11.1 67.1 all-gather.4
  151.6 60.2 all-gather.6
  398.6 92.2 reduce-scatter.1
where the time goes:
time: 500 us; the launch traced here: 499 us
  waiting for transfers between devices  175 us (35%)
  local copies, waits for them, and re-layouts  143 us (29%)
  other arithmetic  68.6 us (14%)
  blocking collectives  53.6 us (11%)
  matrix products  28.2 us (6%)
  between operations  14.8 us (3%)
  starting transfers between devices  8.83 us (2%)
  loops' own time  6.75 us (1%)
    reduce_scatter x1, waiting for transfers between devices, on_device(): lax.psum_scatter(expert_part.astype(jnp.bfloat16), 'tensor', scatter_dime...  90.7 us
    ppermute x5, waiting for transfers between devices, partner(): return lax.ppermute(value, axis, pairs)  53.9 us
    scatter-add x1, other arithmetic, expert_term(): summed = jnp.zeros((row_count + 1, model_width), jnp.float32).at[slot_tab...  46.6 us
    unnamed x33, local copies, waits for them, and re-layouts  45.8 us
    gather x3, local copies, waits for them, and re-layouts, expert_term(): slot_share = jnp.take_along_axis(padded_share.T, slot_table, axis=1)  40.6 us
    all_gather x1, waiting for transfers between devices, on_device(): all_rows = lax.all_gather(normed, 'tensor', axis=0, tiled=True)  30.3 us
    all_gather x1, blocking collectives, on_device(): lax.all_gather(route_weights, 'tensor', axis=0, tiled=True)  30.1 us
    gather x1, local copies, waits for them, and re-layouts, expert_term(): picked = padded_in[slot_table]  28.9 us
  transfers between devices with their start and end apart: 8, of which 7 were waited for; matrix products, arithmetic and copies ran while one was open for 19% of the time, Pallas kernels for 0%

commit v1 on v0

--- a/solution.py
+++ b/solution.py
@@ -159,7 +159,15 @@
     w_attn_out = by_quarter[:, :, qkv_width:].reshape(model_width, GQ * HD)
     w_query = w_group[:, : GQ * HD]
     w_pairs = w_group[:, GQ * HD :]
-    all_rows = lax.all_gather(normed, "tensor", axis=0, tiled=True)
+    all_rows = jnp.concatenate(
+        lax.all_to_all(
+            jnp.stack([normed for _ in range(lax.psum(1, axis_name="tensor"))], 0),
+            concat_axis=0,
+            split_axis=0,
+            axis_name="tensor",
+        ),
+        0,
+    )
     own_rows = lax.dynamic_slice_in_dim(all_rows, quarter_index * rows_quarter, rows_quarter, 0)
     key_values = project_pairs(all_rows, w_pairs, positions)
     kv_block = lax.dynamic_slice_in_dim(key_values, quarter_index * rows_quarter, rows_quarter, 0)

time: 500 us -> 544 us (1.088)
  waiting for transfers between devices: 175 us -> 209 us
  starting transfers between devices: 8.83 us -> 17.2 us
    ppermute x5, waiting for transfers between devices: 53.9 us -> 117 us  [partner(): return lax.ppermute(value, axis, pairs)]
    all_gather x1 -> x0, waiting for transfers between devices: 30.3 us -> none  [on_device(): all_rows = lax.all_gather(normed, 'tensor', axis=0, tiled=True)]
    all_to_all x0 -> x1, starting transfers between devices: none -> 7.8 us  [on_device(): lax.all_to_all(jnp.stack([normed for _ in range(lax.psum(1, axis_name='te...]
    unnamed x33 -> x39, local copies, waits for them, and re-layouts: 45.8 us -> 45.8 us
  transfers between devices with their start and end apart: 8 -> 8, of which waited for: 7 -> 6; matrix products, arithmetic and copies ran while one was open for 19% -> 17% of each run, Pallas kernels for 0% -> 0%
where the time goes in v1:
time: 544 us; the launch traced here: 543 us
  waiting for transfers between devices  209 us (38%)
  local copies, waits for them, and re-layouts  146 us (27%)
  other arithmetic  64.9 us (12%)
  blocking collectives  55.5 us (10%)
  matrix products  28.2 us (5%)
  starting transfers between devices  17.2 us (3%)
  between operations  15.2 us (3%)
  loops' own time  6.79 us (1%)
    ppermute x5, waiting for transfers between devices, partner(): return lax.ppermute(value, axis, pairs)  117 us
    reduce_scatter x1, waiting for transfers between devices, on_device(): lax.psum_scatter(expert_part.astype(jnp.bfloat16), 'tensor', scatter_dime...  92.4 us
    scatter-add x1, other arithmetic, expert_term(): summed = jnp.zeros((row_count + 1, model_width), jnp.float32).at[slot_tab...  46.6 us
    unnamed x39, local copies, waits for them, and re-layouts  45.8 us
    gather x3, local copies, waits for them, and re-layouts, expert_term(): slot_share = jnp.take_along_axis(padded_share.T, slot_table, axis=1)  40.6 us
    all_gather x1, blocking collectives, on_device(): lax.all_gather(route_weights, 'tensor', axis=0, tiled=True)  31.4 us
    gather x1, local copies, waits for them, and re-layouts, expert_term(): picked = padded_in[slot_table]  28.9 us
    all_gather x1, blocking collectives, on_device(): lax.all_gather(routes, 'tensor', axis=0, tiled=True)  24.1 us
  transfers between devices with their start and end apart: 8, of which 6 were waited for; matrix products, arithmetic and copies ran while one was open for 17% of the time, Pallas kernels for 0%

profile of v1, /device:TPU:2, one launch (start us, length us, event | category | flops | bytes accessed | tf_op | source)
XLA Modules:
  0.0 543.4 jit_solution(6975249027761952776)
XLA Ops:
  9.5 3.4 stack.2
  12.8 7.8 %all-to-all-start = ((bf16[32,64,1536]{2,1,0:T(8,128)(2,1)}), bf16[32,64,1536]{2,1,0:T(8,128)(2,1)}, u32[]{:S(2)}, u32[]{:S(2)}) async-start(bf16[32,64,1536]{2,1,0:T(8,128)(2,1)} %stack.2), calls=%async_computation | async-start | bytes 12582912 | tf_op jit(solution)/shard_map/all_to_all | solution.py:163
  20.7 1.6 collective-permute-start
  24.1 75.2 %collective-permute-done = bf16[1536,128]{0,1:T(8,128)(2,1)S(1)} collective-permute-done((bf16[1536,128]{0,1:T(8,128)(2,1)S(1)}, bf16[1536,128]{0,1:T(8,128)(2,1)S(1)}, u32[]{:S(2)}, u32[]{:S(2)}) %collective-permute-start) | collective-permute-done | bytes 393248 | tf_op jit(solution)/shard_map/ppermute | solution.py:20
  99.4 2.8 collective-permute-start.1
  102.4 1.7 multiply_cosine_fusion.1
  104.1 15.8 %collective-permute-done.1 = bf16[1536,256]{0,1:T(8,128)(2,1)S(1)} collective-permute-done((bf16[1536,256]{0,1:T(8,128)(2,1)S(1)}, bf16[1536,256]{0,1:T(8,128)(2,1)S(1)}, u32[]{:S(2)}, u32[]{:S(2)}) %collective-permute-start.1) | collective-permute-done | bytes 786464 | tf_op jit(solution)/shard_map/ppermute | solution.py:20
  121.2 2.1 fusion.12
  123.2 4.9 fusion.25
  132.4 2.1 copy.61
  136.2 14.7 %while.59 = (s32[]{:T(128)}, bf16[2,256,192]{1,2,0:T(8,128)(2,1)}, s32[2]{0:T(128)S(1)}, s32[]{:T(128)}, s32[2048]{0:T(1024)S(1)}, /*index=5*/bf16[3,512,64]{2,1...) while((s32[]{:T(128)}, bf16[2,256,192]{1,2,0:T(8,128)(2,1)}, ...), condition=%wide.region_8.9_spmd, body=%wide.region_3.8_spmd.sunk | while | flops 104007976 | bytes 10327068 | solution.py:230
  140.7 2.0 while.60
  148.1 2.0 while.60
  151.8 1.7 fusion.47
  153.5 1.7 copy-done.1
  155.3 2.7 collective-permute-start.2
  158.0 17.1 %collective-permute-done.2 = bf16[256,1536]{1,0:T(8,128)(2,1)} collective-permute-done((bf16[256,1536]{1,0:T(8,128)(2,1)S(1)}, bf16[256,1536]{1,0:T(8,128)(2,1)}, u32[]{:S(2)}, u32[]{:S(2)}) %collective-permute-start.2) | collective-permute-done | bytes 786464 | tf_op jit(solution)/shard_map/ppermute | solution.py:20
  175.1 2.5 convert_add_fusion
  178.4 2.0 collective-permute-start.3
  180.4 7.4 %collective-permute-done.3 = bf16[128,1536]{1,0:T(8,128)(2,1)} collective-permute-done((bf16[128,1536]{1,0:T(8,128)(2,1)}, bf16[128,1536]{1,0:T(8,128)(2,1)}, u32[]{:S(2)}, u32[]{:S(2)}) %collective-permute-start.3) | collective-permute-done | bytes 393248 | tf_op jit(solution)/shard_map/ppermute | solution.py:20
  191.9 31.4 %all-gather.1 = bf16[32,64,8]{1,2,0:T(8,128)(2,1)S(1)} all-gather(bf16[1,64,8]{1,2,0:T(8,128)(2,1)S(1)} %bitcast.111), channel_id=1, replica_groups=mesh['dp'=8,'tensor'=32] {'tensor'}, dimensions={0}, use_global_device_ids=true | all-gather | bytes 33792 | tf_op jit(solution)/shard_map/all_gather | solution.py:252
  223.4 24.1 %all-gather = s32[32,64,8]{1,2,0:T(8,128)S(1)} all-gather(s32[1,64,8]{1,2,0:T(8,128)S(1)} %bitcast.110), channel_id=1, replica_groups=mesh['dp'=8,'tensor'=32] {'tensor'}, dimensions={0}, use_global_device_ids=true | all-gather | bytes 67584 | tf_op jit(solution)/shard_map/all_gather | solution.py:251
  253.4 37.9 %scatter_custom_fusion.1 = s32[4085]{0:T(1024)S(1)} fusion(s32[10240]{0:T(1024)S(1)} %reshape.406, s32[10240]{0:T(1024)S(1)} %reshape.408, s32[]{:T(128)} %constant.223.clone.1), kind=kCustom, calls=%fused_computation.101 | custom fusion | bytes 16344
  292.8 40.4 %gather_fusion.1 = f32[4080]{0:T(1024)S(1)} fusion(f32[5,2049]{0,1:T(8,128)S(1)} %pad_bitcast_fusion, s32[4080]{0:T(1024)S(1)} %reshape.392), kind=kCustom, calls=%fused_computation.1 | custom fusion | bytes 65280 | tf_op jit(solution)/shard_map/jit(take_along_axis)/gather | solution.py:113
  333.6 5.8 %concatenate.56 = bf16[2049,1536]{1,0:T(8,128)(2,1)} pad(bf16[2048,1536]{1,0:T(8,128)(2,1)} %all-gather.4.cloned.1.call-done, bf16[]{:T(256)} %constant.215.clone.1), padding=0_1x0_0 | pad | bytes 12585986 | tf_op jit(solution)/shard_map/concatenate | solution.py:110
  339.4 28.9 %gather_fusion = bf16[4080,1536]{1,0:T(8,128)(2,1)} fusion(bf16[2049,1536]{1,0:T(8,128)(2,1)} %concatenate.56, s32[4096]{0:T(1024)S(1)} %pad_clamp_fusion), kind=kCustom, calls=%fused_computation | custom fusion | bytes 25083840 | tf_op jit(solution)/shard_map/gather | solution.py:112
  368.4 7.6 %fusion.48 = f32[5,816,256]{2,1,0:T(8,128)S(1)} fusion(bf16[5,816,1536]{2,1,0:T(8,128)(2,1)} %bitcast.95, bf16[5,1536,256]{2,1,0:T(8,128)(2,1)} %param.22), kind=kOutput, calls=%fused_computation.117 | convolution fusion | flops 3208642560 | bytes 20643840 | tf_op jit(solution)/shard_map/ecd,edf->ecf/dot_general | solution.py:114
  376.0 10.1 %convolution_multiply_fusion = f32[5,816,1536]{2,1,0:T(8,128)} fusion(bf16[5,128,1536]{2,1,0:T(8,128)(2,1)S(1)} %copy-done, f32[5,816]{1,0:T(8,128)S(1)} %and_select_fusion, f32[5,816,256]{2,1,0:T(8,128)S(1)} %fusion.48), kind=kOutput, calls=%fused_computation.22 | convolution fusion | flops 1613721600 | bytes 31227840 | tf_op jit(solution)/shard_map/ecf,efd->ecd/dot_general | solution.py:119
  386.1 46.6 %scatter_custom_fusion = f32[2049,1536]{1,0:T(8,128)} fusion(s32[4080]{0:T(1024)S(1)} %bitcast.108, f32[4080,1536]{1,0:T(8,128)} %bitcast.93, f32[]{:T(128)} %constant.216.clone.1), kind=kCustom, calls=%fused_computation.24 | custom fusion | flops 6266880 | bytes 12589568 | tf_op jit(solution)/shard_map/scatter-add | solution.py:125
  432.7 8.0 %slice.188 = bf16[2048,1536]{1,0:T(8,128)(2,1)} slice(f32[2049,1536]{1,0:T(8,128)} %scatter_custom_fusion), slice={[0:2048], [0:1536]} | slice | bytes 12582912 | tf_op jit(solution)/shard_map/slice | solution.py:127
  442.5 92.4 %reduce-scatter.2.cloned.1.call-done = bf16[64,1536]{1,0:T(8,128)(2,1)} async-done(((bf16[2048,1536]{1,0:T(8,128)(2,1)}), bf16[64,1536]{1,0:T(8,128)(2,1)}) %reduce-scatter.2.cloned.1.call-update) | async-done | bytes 196624 | tf_op jit(solution)/shard_map/reduce_scatter | solution.py:263
  534.9 1.7 fusion.24
  (165 shorter events, 34.1 us)
Async XLA Ops:
  7.2 368.8 %copy-start = (bf16[5,128,1536]{2,1,0:T(8,128)(2,1)S(1)}, bf16[5,128,1536]{2,1,0:T(8,128)(2,1)}, u32[]{:S(2)}) copy-start(bf16[5,128,1536]{2,1,0:T(8,128)(2,1)} %param.23) | copy-start | bytes 5898244
  12.8 7.9 %copy-start.8 = (bf16[1536,80]{0,1:T(8,128)(2,1)S(1)}, bf16[1536,80]{0,1:T(8,128)(2,1)}, u32[]{:S(2)}) copy-start(bf16[1536,80]{0,1:T(8,128)(2,1)} %param.19) | copy-start | bytes 737284
  12.8 7.9 %copy-start.9 = (bf16[1536,48]{0,1:T(8,128)(2,1)S(1)}, bf16[1536,48]{0,1:T(8,128)(2,1)}, u32[]{:S(2)}) copy-start(bf16[1536,48]{0,1:T(8,128)(2,1)} %param.20) | copy-start | bytes 442372
  12.8 9.5 %copy-start.12 = (s32[2048]{0:T(1024)S(1)}, s32[2048]{0:T(1024)}, u32[]{:S(2)}) copy-start(s32[2048]{0:T(1024)} %param.15) | copy-start | bytes 24580
  12.8 108.3 %all-to-all-start = ((bf16[32,64,1536]{2,1,0:T(8,128)(2,1)}), bf16[32,64,1536]{2,1,0:T(8,128)(2,1)}, u32[]{:S(2)}, u32[]{:S(2)}) async-start(bf16[32,64,1536]{2,1,0:T(8,128)(2,1)} %stack.2), calls=%async_computation | async-start | bytes 12582912 | tf_op jit(solution)/shard_map/all_to_all | solution.py:163
  20.6 313.0 %all-gather.4.cloned.1.call-start = ((), (), s32[]{:S(2)}) async-start(), calls=%async_computation.2 | async-start | bytes 6488064 | tf_op jit(solution)/shard_map/all_gather | solution.py:250
  20.7 78.5 %collective-permute-start = (bf16[1536,128]{0,1:T(8,128)(2,1)S(1)}, bf16[1536,128]{0,1:T(8,128)(2,1)S(1)}, u32[]{:S(2)}, u32[]{:S(2)}) collective-permute-start(bf16[1536,128]{0,1:T(8,128)(2,1)S(1)} %pad_maximum_fusion.1), channel_id=1, source_target_pairs={{0,8},{1,9},{2,10},{3,11},{4,12},{5,13},{6,14},{7,15},{8,0},{9,1},... | collective-permute-start | bytes 1179656 | tf_op jit(solution)/shard_map/ppermute | solution.py:20
  99.4 20.6 %collective-permute-start.1 = (bf16[1536,256]{0,1:T(8,128)(2,1)S(1)}, bf16[1536,256]{0,1:T(8,128)(2,1)S(1)}, u32[]{:S(2)}, u32[]{:S(2)}) collective-permute-start(bf16[1536,256]{0,1:T(8,128)(2,1)S(1)} %maximum_select_fusion.1), channel_id=1, source_target_pairs={{0,16},{1,17},{2,18},{3,19},{4,20},{5,21},{6,22},{7,23},{8,24},{9,... | collective-permute-start | bytes 2359304 | tf_op jit(solution)/shard_map/ppermute | solution.py:20
  128.2 2.0 copy-start.2
  130.2 0.7 copy-start.4
  140.7 2.1 copy-start.10
  142.9 0.7 copy-start.11
  148.0 2.1 copy-start.10
  150.2 0.7 copy-start.11
  153.5 1.7 copy-start.1
  155.3 19.8 %collective-permute-start.2 = (bf16[256,1536]{1,0:T(8,128)(2,1)S(1)}, bf16[256,1536]{1,0:T(8,128)(2,1)}, u32[]{:S(2)}, u32[]{:S(2)}) collective-permute-start(bf16[256,1536]{1,0:T(8,128)(2,1)S(1)} %select_convert_fusion), channel_id=1, source_target_pairs={{0,4},{1,5},{2,6},{3,7},{4,0},{5,1},{6,2},{7,3},{8,12},{9,13},{10,... | collective-permute-start | bytes 2359304 | tf_op jit(solution)/shard_map/ppermute | solution.py:20
  178.4 9.4 %collective-permute-start.3 = (bf16[128,1536]{1,0:T(8,128)(2,1)}, bf16[128,1536]{1,0:T(8,128)(2,1)}, u32[]{:S(2)}, u32[]{:S(2)}) collective-permute-start(bf16[128,1536]{1,0:T(8,128)(2,1)} %select_convert_fusion.1), channel_id=1, source_target_pairs={{0,2},{1,3},{2,0},{3,1},{4,6},{5,7},{6,4},{7,5},{8,10},{9,11},{10,... | collective-permute-start | bytes 1179656 | tf_op jit(solution)/shard_map/ppermute | solution.py:20
  180.4 10.3 %copy-start.6 = (bf16[64,1536]{1,0:T(8,128)(2,1)S(1)}, bf16[64,1536]{1,0:T(8,128)(2,1)}, u32[]{:S(2)}) copy-start(bf16[64,1536]{1,0:T(8,128)(2,1)} %param.14) | copy-start | bytes 589828
  180.4 10.6 %copy-start.13 = (f32[1536]{0:T(1024)S(1)}, f32[1536]{0:T(1024)}, u32[]{:S(2)}) copy-start(f32[1536]{0:T(1024)} %param.21) | copy-start | bytes 18436
  180.4 11.4 %copy-start.15 = (bf16[64,8]{0,1:T(8,128)(2,1)S(1)}, bf16[64,8]{0,1:T(8,128)(2,1)}, u32[]{:S(2)}) copy-start(bf16[64,8]{0,1:T(8,128)(2,1)} %param.17) | copy-start | bytes 3076
  188.9 34.4 %copy-start.14 = (s32[64,8]{0,1:T(8,128)S(1)}, s32[64,8]{0,1:T(8,128)}, u32[]{:S(2)}) copy-start(s32[64,8]{0,1:T(8,128)} %param.16) | copy-start | bytes 6148
  188.9 60.9 %copy-start.17 = (s32[2]{0:T(128)S(1)}, s32[2]{0:T(128)}, u32[]{:S(2)}) copy-start(s32[2]{0:T(128)} %constant.248) | copy-start | bytes 28
  189.0 60.9 %copy-start.16 = (s32[2]{0:T(128)S(1)}, s32[2]{0:T(128)}, u32[]{:S(2)}) copy-start(s32[2]{0:T(128)} %constant.251) | copy-start | bytes 28
  189.0 1.7 collective-permute-start.4
  190.9 344.0 %copy-start.7 = (bf16[64,1536]{1,0:T(8,128)(2,1)}, bf16[64,1536]{1,0:T(8,128)(2,1)S(1)}, u32[]{:S(2)}) copy-start(bf16[64,1536]{1,0:T(8,128)(2,1)S(1)} %get-tuple-element.314) | copy-start | bytes 589828
  191.8 343.1 %reduce-scatter.2.cloned.1.call-start = ((), (), s32[]{:S(2)}) async-start(), calls=%async_computation.3 | async-start | bytes 6488064 | tf_op jit(solution)/shard_map/reduce_scatter | solution.py:263
  440.7 0.9 copy-start.3
  440.7 1.0 copy-start.5
Sparse Core Ops, SparseCore 0:
  191.9 63.8 all-gather.3
  440.9 94.0 reduce-scatter.1
